TPU v7x, 256 devices: a whole 4x4x8 slice. The times are simulated.
256 devices in a mesh: node: 64 (over z, y, core), state: 4 (over x).
Axes of the slice: x: 4, y: 4, z: 8, core: 2. Of those that a mesh axis runs over, the one named last changes fastest.
Arguments:
- block: bfloat16 [64, 2097152], P('state', 'node'), may hold values from -6 to 6
- connectivity: int32 [125, 32768], P(None, 'node'), may hold values from 0 to 49151, as said below
- potential: float32 [125, 32768], P(None, 'node'), may hold values from 0.1 to 3
- cell_matrix: bfloat16 [125, 125], replicated, as said below
Outputs:
- orthonormal: bfloat16 [64, 2097152], P('state', 'node')
- factor: float32 [64, 64], replicated
Inputs may be any that keep to these rules, and one draw needn't show every extreme that they name: `connectivity`: in each slab, numbers below 8192 are the previous slab's last 8192 nodes and numbers from 40960 on are the next slab's first nodes. The numbers of the slab's k-th cell (k from 0) lie in k * 96 to k * 96 + 2 * 96 - 1, those of its last cell in k * 96 to k * 96 + 95; each cell reaches the lower end of its range. `cell_matrix`: Symmetric.
All inputs are finite; a program needn't handle non-finite values.
Results may differ from a plain program's by a relative error of at most 0.015.
Values may be sent and summed in bfloat16 or wider, within the bound.
No kernel may reach another device: no remote copies, remote signals or barrier semaphores. Data moves between devices by JAX's collectives and lax.ppermute only.
A program may use at most 64 MiB of HBM per device.

v0:
```python
import jax
import jax.numpy as jnp
from jax import lax
from jax.sharding import PartitionSpec as P

CENTER = 3.0
HALF_WIDTH = 3.0


def extended(block, sides, width):
    for axis, dim in sides:
        count = lax.axis_size(axis)
        forward = [(i, i + 1) for i in range(count - 1)]
        backward = [(target, source) for source, target in forward]
        low = lax.ppermute(
            lax.slice_in_dim(block, block.shape[dim] - width, None, axis=dim), axis, forward
        )
        high = lax.ppermute(lax.slice_in_dim(block, 0, width, axis=dim), axis, backward)
        block = jnp.concatenate([low, block, high], axis=dim)
    return block


def passed_along(block, axis, distance):
    devices = range(lax.axis_size(axis))
    route = [(i - distance, i) for i in devices if i - distance in devices]
    return lax.ppermute(block, axis, route)


def cell_terms(window, connectivity, potential, cell_matrix):
    states = window.shape[0]
    cells = connectivity.shape[1]
    stride = window.shape[1] // cells
    segments = window.reshape(states, cells, stride)
    following = jnp.concatenate(
        [segments[:, 1:], jnp.zeros((states, 1, stride), segments.dtype)], axis=1
    )
    paired = jnp.concatenate([segments, following], axis=2)
    offsets = jnp.arange(cells, dtype=jnp.int32) * stride
    local_links = connectivity - offsets[None, :]
    columns = jnp.arange(2 * stride, dtype=jnp.int32)
    group = min(cells, 128)
    pieces = []
    for first_cell in range(0, cells, group):
        links = local_links[:, first_cell : first_cell + group]
        picker = links[:, :, None] == columns[None, None, :]
        picker_half = picker.astype(jnp.bfloat16)
        part_pair = paired[:, first_cell : first_cell + group]
        values = jnp.einsum(
            "skn,jkn->sjk", part_pair, picker_half, preferred_element_type=jnp.float32
        )
        mixed = jnp.einsum(
            "ij,sjk->sik",
            cell_matrix,
            values.astype(jnp.bfloat16),
            preferred_element_type=jnp.float32,
        )
        mixed = mixed + potential[None, :, first_cell : first_cell + group] * values
        spread = jnp.einsum(
            "sjk,jkn->skn", mixed, picker.astype(jnp.float32), precision=lax.Precision.HIGHEST
        )
        pieces.append(spread)
    spread = jnp.concatenate(pieces, axis=1)
    lower = spread[:, :, :stride]
    upper = spread[:, :, stride:]
    shifted = jnp.concatenate([jnp.zeros((states, 1, stride), jnp.float32), upper[:, :-1]], axis=1)
    return (lower + shifted).reshape(states, cells * stride)


def operate(field, connectivity, potential, cell_matrix):
    owned = field.shape[1]
    margin = owned // 4
    window = extended(field, (("node", 1),), margin)
    summed = cell_terms(window, connectivity, potential, cell_matrix)
    result = summed[:, margin : margin + owned]
    from_above = passed_along(summed[:, :margin].astype(jnp.bfloat16), "node", -1).astype(
        jnp.float32
    )
    from_below = passed_along(summed[:, margin + owned :].astype(jnp.bfloat16), "node", 1).astype(
        jnp.float32
    )
    result = result.at[:, owned - margin :].add(from_above)
    result = result.at[:, :margin].add(from_below)
    return result


def factorize(intersection):
    factor = jnp.linalg.cholesky(intersection)
    identity = jnp.eye(intersection.shape[0], dtype=factor.dtype)
    inverse = lax.linalg.triangular_solve(factor, identity, left_side=True, lower=True).astype(
        jnp.bfloat16
    )
    return (factor, inverse)


def per_device(block, connectivity, potential, cell_matrix):
    start = block.astype(jnp.float32)
    image = operate(block, connectivity, potential, cell_matrix)
    first = ((image - CENTER * start) / HALF_WIDTH).astype(jnp.bfloat16)
    image = operate(first, connectivity, potential, cell_matrix)
    second = (2.0 * (image - CENTER * first.astype(jnp.float32)) / HALF_WIDTH - start).astype(
        jnp.bfloat16
    )
    total_nodes = block.shape[1] * lax.axis_size("node")
    panel = lax.all_gather(second, "state", axis=0, tiled=True)
    partial_intersection = jnp.einsum("an,bn->ab", panel, panel, preferred_element_type=jnp.float32)
    intersection = lax.psum(partial_intersection, "node") / total_nodes
    factor, inverse = factorize(intersection)
    rows = second.shape[0]
    mine = lax.dynamic_slice_in_dim(inverse, lax.axis_index("state") * rows, rows, 0)
    orthonormal = jnp.dot(mine, panel, preferred_element_type=jnp.float32).astype(jnp.bfloat16)
    return (orthonormal, factor)


def solution(mesh):
    return jax.shard_map(
        per_device,
        mesh=mesh,
        in_specs=(P("state", "node"), P(None, "node"), P(None, "node"), P()),
        out_specs=(P("state", "node"), P()),
        check_vma=False,
    )
```

profile of v0, /device:TPU:2, one launch (start us, length us, event | category | flops | bytes accessed | tf_op | source)
XLA Modules:
  0.0 566.9 jit_solution(16091128970053678684)
XLA Ops:
  8.4 1.8 collective-permute-start
  10.1 1.3 collective-permute-start.1
  16.8 3.2 reshape.132
  20.0 1.4 copy.18
  21.7 2.8 fusion.34
  24.5 3.0 fusion.123
  28.4 4.3 fusion.122
  33.6 4.3 fusion.121
  38.2 1.5 copy.37
  39.8 4.2 fusion.120
  44.3 1.4 copy.39
  45.8 11.6 %fusion.42 = f32[16,128,192]{2,0,1:T(8,128)S(1)} fusion(s32[125,128]{0,1:T(8,128)S(1)} %copy.16, f32[16,128,125]{2,0,1:T(8,128)S(1)} %copy.33, f32[16,125,128]{1,0,2:T(8,128)} %get-tuple-element.75, f32[125,128]{0,1:T(8,128)} %copy.19), kind=kOutput, calls=%fused_computation.59 | convolution fusion | flops 593408000 | bytes 3748864 | tf_op jit(solution)/shard_map/sjk,jkn->skn/dot_general | solution.py:58
  57.4 9.9 %fusion.44 = f32[16,128,192]{2,0,1:T(8,128)S(1)} fusion(s32[125,128]{0,1:T(8,128)S(1)} %copy-done.11, f32[16,128,125]{2,0,1:T(8,128)S(1)} %copy.35, f32[16,125,128]{1,0,2:T(8,128)S(1)} %copy-done.19, f32[125,128]{0,1:T(8,128)S(1)} %copy-done.14), kind=kOutput, calls=%fused_computation.61 | convolution fusion | flops 593408000 | bytes 3748864 | tf_op jit(solution)/shard_map/sjk,jkn->skn/dot_general | solution.py:58
  67.3 10.0 %fusion.46 = f32[16,128,192]{2,0,1:T(8,128)S(1)} fusion(s32[125,128]{0,1:T(8,128)S(1)} %copy.22, f32[16,128,125]{2,0,1:T(8,128)S(1)} %copy-done.7, f32[16,125,128]{1,0,2:T(8,128)S(1)} %copy-done.20, f32[125,128]{0,1:T(8,128)S(1)} %copy.23), kind=kOutput, calls=%fused_computation.63 | convolution fusion | flops 593408000 | bytes 3748864 | tf_op jit(solution)/shard_map/sjk,jkn->skn/dot_general | solution.py:58
  77.3 9.8 %fusion.48 = f32[16,128,192]{2,0,1:T(8,128)S(1)} fusion(s32[125,128]{0,1:T(8,128)S(1)} %copy.24, f32[16,128,125]{2,0,1:T(8,128)S(1)} %copy-done.9, f32[16,125,128]{1,0,2:T(8,128)S(1)} %copy-done.21, f32[125,128]{0,1:T(8,128)S(1)} %copy.25), kind=kOutput, calls=%fused_computation.65 | convolution fusion | flops 593408000 | bytes 3748864 | tf_op jit(solution)/shard_map/sjk,jkn->skn/dot_general | solution.py:58
  88.2 2.3 fusion.37
  90.5 3.2 copy.26
  93.8 4.0 reshape.133
  98.0 1.3 collective-permute-start.2
  100.0 6.8 %collective-permute-start.3 = (bf16[16,8192]{1,0:T(8,128)(2,1)S(1)}, bf16[16,8192]{1,0:T(8,128)(2,1)S(1)}, u32[]{:S(2)}, u32[]{:S(2)}) collective-permute-start(bf16[16,8192]{1,0:T(8,128)(2,1)S(1)} %get-tuple-element.54), channel_id=1, source_target_pairs={{0,4},{4,8},{8,12},{12,16},{16,20},{20,24},{24,28},{28,32},{32,36}... | collective-permute-start | bytes 786440 | tf_op jit(solution)/shard_map/ppermute | solution.py:26
  109.2 5.8 %collective-permute-start.4 = (bf16[16,8192]{1,0:T(8,128)(2,1)S(1)}, bf16[16,8192]{1,0:T(8,128)(2,1)S(1)}, u32[]{:S(2)}, u32[]{:S(2)}) collective-permute-start(bf16[16,8192]{1,0:T(8,128)(2,1)S(1)} %get-tuple-element.56), channel_id=1, source_target_pairs={{0,4},{4,8},{8,12},{12,16},{16,20},{20,24},{24,28},{28,32},{32,36}... | collective-permute-start | bytes 786440 | tf_op jit(solution)/shard_map/ppermute | solution.py:15
  115.0 1.3 collective-permute-start.5
  116.3 4.1 collective-permute-done.5
  121.7 3.2 reshape.134
  124.9 1.4 copy.28
  126.6 3.0 fusion.35
  129.6 3.0 fusion.127
  132.7 3.0 fusion.126
  135.7 3.0 fusion.125
  138.7 3.0 fusion.124
  142.0 1.5 copy.41
  143.8 1.4 copy.43
  147.0 11.7 %fusion.43 = f32[16,128,192]{2,0,1:T(8,128)S(1)} fusion(s32[125,128]{0,1:T(8,128)S(1)} %copy.16, f32[16,128,125]{2,0,1:T(8,128)} %copy.41, f32[16,125,128]{1,0,2:T(8,128)} %get-tuple-element.83, f32[125,128]{0,1:T(8,128)} %copy.19), kind=kOutput, calls=%fused_computation.60 | convolution fusion | flops 593408000 | bytes 3748864 | tf_op jit(solution)/shard_map/sjk,jkn->skn/dot_general | solution.py:58
  158.8 9.9 %fusion.45 = f32[16,128,192]{2,0,1:T(8,128)S(1)} fusion(s32[125,128]{0,1:T(8,128)S(1)} %copy-done.13, f32[16,128,125]{2,0,1:T(8,128)S(1)} %copy-done.8, f32[16,125,128]{1,0,2:T(8,128)S(1)} %copy-done.18, f32[125,128]{0,1:T(8,128)S(1)} %copy-done.15), kind=kOutput, calls=%fused_computation.62 | convolution fusion | flops 593408000 | bytes 3748864 | tf_op jit(solution)/shard_map/sjk,jkn->skn/dot_general | solution.py:58
  168.7 10.0 %fusion.47 = f32[16,128,192]{2,0,1:T(8,128)S(1)} fusion(s32[125,128]{0,1:T(8,128)S(1)} %copy.22, f32[16,128,125]{2,0,1:T(8,128)S(1)} %copy.45, f32[16,125,128]{1,0,2:T(8,128)S(1)} %copy-done.17, f32[125,128]{0,1:T(8,128)S(1)} %copy.23), kind=kOutput, calls=%fused_computation.64 | convolution fusion | flops 593408000 | bytes 3748864 | tf_op jit(solution)/shard_map/sjk,jkn->skn/dot_general | solution.py:58
  178.7 9.8 %fusion.49 = f32[16,128,192]{2,0,1:T(8,128)S(1)} fusion(s32[125,128]{0,1:T(8,128)S(1)} %copy.24, f32[16,128,125]{2,0,1:T(8,128)S(1)} %copy.47, f32[16,125,128]{1,0,2:T(8,128)S(1)} %copy-done.16, f32[125,128]{0,1:T(8,128)S(1)} %copy.25), kind=kOutput, calls=%fused_computation.66 | convolution fusion | flops 593408000 | bytes 3748864 | tf_op jit(solution)/shard_map/sjk,jkn->skn/dot_general | solution.py:58
  189.6 2.3 fusion.36
  192.0 3.2 copy.29
  195.2 4.0 reshape.135
  199.4 1.4 collective-permute-start.6
  201.0 7.3 %collective-permute-start.7 = (bf16[16,8192]{1,0:T(8,128)(2,1)S(1)}, bf16[16,8192]{1,0:T(8,128)(2,1)S(1)}, u32[]{:S(2)}, u32[]{:S(2)}) collective-permute-start(bf16[16,8192]{1,0:T(8,128)(2,1)S(1)} %get-tuple-element.52), channel_id=1, source_target_pairs={{0,4},{4,8},{8,12},{12,16},{16,20},{20,24},{24,28},{28,32},{32,36}... | collective-permute-start | bytes 786440 | tf_op jit(solution)/shard_map/ppermute | solution.py:26
  210.3 1.4 fusion.41
  211.7 75.3 %all-gather.2.cloned.1.call-done = bf16[64,32768]{1,0:T(8,128)(2,1)} async-done(((bf16[16,32768]{1,0:T(8,128)(2,1)}), bf16[64,32768]{1,0:T(8,128)(2,1)}) %all-gather.2.cloned.1.call-update) | async-done | bytes 4194320 | tf_op jit(solution)/shard_map/all_gather | solution.py:104
  287.0 4.7 fusion.128
  291.7 251.0 %psum.7 = f32[64,64]{0,1:T(8,128)S(1)} all-reduce(f32[64,64]{0,1:T(8,128)S(1)} %fusion.128), channel_id=1, replica_groups=mesh['node'=64,'state'=4] {'node'}, use_global_device_ids=true, to_apply=%region_1.0 | all-reduce | flops 4096 | bytes 32768 | tf_op jit(solution)/shard_map/psum | solution.py:106
  542.8 5.8 %cholesky.17 = f32[64,64]{1,0:T(8,128)S(1)} custom-call(f32[64,64]{1,0:T(8,128)S(1)} %fusion.104), custom_call_target="Cholesky" | custom-call | tf_op jit(solution)/shard_map/jit(cholesky)/cholesky | solution.py:87
  550.6 4.9 custom-call.6
  555.8 3.8 convolution_convert_fusion
  (104 shorter events, 23.2 us)
Async XLA Ops:
  7.2 20.4 %copy-start = (bf16[125,125]{1,0:T(8,128)(2,1)S(1)}, bf16[125,125]{1,0:T(8,128)(2,1)}, u32[]{:S(2)}) copy-start(bf16[125,125]{1,0:T(8,128)(2,1)} %param.15) | copy-start | bytes 93754
  7.2 8.4 %copy-start.1 = (bf16[16,32768]{1,0:T(8,128)(2,1)S(1)}, bf16[16,32768]{1,0:T(8,128)(2,1)}, u32[]{:S(2)}) copy-start(bf16[16,32768]{1,0:T(8,128)(2,1)} %param.12) | copy-start | bytes 3145732
  7.2 279.8 %all-gather.2.cloned.1.call-start = ((), (), s32[]{:S(2)}) async-start(), calls=%async_computation | async-start | bytes 5242880 | tf_op jit(solution)/shard_map/all_gather | solution.py:104
  8.4 7.1 %collective-permute-start = (bf16[16,8192]{1,0:T(8,128)(2,1)S(1)}, bf16[16,8192]{1,0:T(8,128)(2,1)S(1)}, u32[]{:S(2)}, u32[]{:S(2)}) collective-permute-start(bf16[16,8192]{1,0:T(8,128)(2,1)S(1)} %get-tuple-element.58), channel_id=1, source_target_pairs={{0,4},{4,8},{8,12},{12,16},{16,20},{20,24},{24,28},{28,32},{32,36}... | collective-permute-start | bytes 786440 | tf_op jit(solution)/shard_map/ppermute | solution.py:15
  10.1 5.4 collective-permute-start.1
  14.4 14.1 %copy-start.10 = (s32[125,128]{0,1:T(8,128)}, s32[125,128]{0,1:T(8,128)S(1)}, u32[]{:S(2)}) copy-start(s32[125,128]{0,1:T(8,128)S(1)} %copy.20) | copy-start | bytes 192004
  24.5 3.0 copy-start.6
  45.8 11.6 %copy-start.11 = (s32[125,128]{0,1:T(8,128)S(1)}, s32[125,128]{0,1:T(8,128)}, u32[]{:S(2)}) copy-start(s32[125,128]{0,1:T(8,128)} %copy-done.10) | copy-start | bytes 192004
  45.8 11.6 %copy-start.14 = (f32[125,128]{0,1:T(8,128)S(1)}, f32[125,128]{0,1:T(8,128)}, u32[]{:S(2)}) copy-start(f32[125,128]{0,1:T(8,128)} %copy.21) | copy-start | bytes 192004
  45.8 11.6 %copy-start.19 = (f32[16,125,128]{1,0,2:T(8,128)S(1)}, f32[16,125,128]{1,0,2:T(8,128)}, u32[]{:S(2)}) copy-start(f32[16,125,128]{1,0,2:T(8,128)} %get-tuple-element.73) | copy-start | bytes 3072004
  57.4 9.9 %copy-start.7 = (f32[16,128,125]{2,0,1:T(8,128)S(1)}, f32[16,128,125]{2,0,1:T(8,128)}, u32[]{:S(2)}) copy-start(f32[16,128,125]{2,0,1:T(8,128)} %copy.37) | copy-start | bytes 3072004
  57.4 9.9 %copy-start.20 = (f32[16,125,128]{1,0,2:T(8,128)S(1)}, f32[16,125,128]{1,0,2:T(8,128)}, u32[]{:S(2)}) copy-start(f32[16,125,128]{1,0,2:T(8,128)} %get-tuple-element.71) | copy-start | bytes 3072004
  67.3 10.0 %copy-start.9 = (f32[16,128,125]{2,0,1:T(8,128)S(1)}, f32[16,128,125]{2,0,1:T(8,128)}, u32[]{:S(2)}) copy-start(f32[16,128,125]{2,0,1:T(8,128)} %copy.39) | copy-start | bytes 3072004
  67.3 10.0 %copy-start.21 = (f32[16,125,128]{1,0,2:T(8,128)S(1)}, f32[16,125,128]{1,0,2:T(8,128)}, u32[]{:S(2)}) copy-start(f32[16,125,128]{1,0,2:T(8,128)} %get-tuple-element.69) | copy-start | bytes 3072004
  98.0 8.9 %collective-permute-start.2 = (bf16[16,8192]{1,0:T(8,128)(2,1)S(1)}, bf16[16,8192]{1,0:T(8,128)(2,1)S(1)}, u32[]{:S(2)}, u32[]{:S(2)}) collective-permute-start(bf16[16,8192]{1,0:T(8,128)(2,1)S(1)} %get-tuple-element.55), channel_id=1, source_target_pairs={{4,0},{8,4},{12,8},{16,12},{20,16},{24,20},{28,24},{32,28},{36,32}... | collective-permute-start | bytes 786440 | tf_op jit(solution)/shard_map/ppermute | solution.py:26
  99.9 8.9 %copy-start.2 = (bf16[16,32768]{1,0:T(8,128)(2,1)S(1)}, bf16[16,32768]{1,0:T(8,128)(2,1)}, u32[]{:S(2)}) copy-start(bf16[16,32768]{1,0:T(8,128)(2,1)} %param.12) | copy-start | bytes 3145732
  100.0 8.0 %collective-permute-start.3 = (bf16[16,8192]{1,0:T(8,128)(2,1)S(1)}, bf16[16,8192]{1,0:T(8,128)(2,1)S(1)}, u32[]{:S(2)}, u32[]{:S(2)}) collective-permute-start(bf16[16,8192]{1,0:T(8,128)(2,1)S(1)} %get-tuple-element.54), channel_id=1, source_target_pairs={{0,4},{4,8},{8,12},{12,16},{16,20},{20,24},{24,28},{28,32},{32,36}... | collective-permute-start | bytes 786440 | tf_op jit(solution)/shard_map/ppermute | solution.py:26
  109.2 11.3 %copy-start.4 = (bf16[16,32768]{1,0:T(8,128)(2,1)}, bf16[16,32768]{1,0:T(8,128)(2,1)S(1)}, u32[]{:S(2)}) copy-start(bf16[16,32768]{1,0:T(8,128)(2,1)S(1)} %fusion.40) | copy-start | bytes 3145732
  109.2 7.1 %collective-permute-start.4 = (bf16[16,8192]{1,0:T(8,128)(2,1)S(1)}, bf16[16,8192]{1,0:T(8,128)(2,1)S(1)}, u32[]{:S(2)}, u32[]{:S(2)}) collective-permute-start(bf16[16,8192]{1,0:T(8,128)(2,1)S(1)} %get-tuple-element.56), channel_id=1, source_target_pairs={{0,4},{4,8},{8,12},{12,16},{16,20},{20,24},{24,28},{28,32},{32,36}... | collective-permute-start | bytes 786440 | tf_op jit(solution)/shard_map/ppermute | solution.py:15
  115.0 5.4 collective-permute-start.5
  129.6 3.0 copy-start.12
  147.0 11.7 %copy-start.8 = (f32[16,128,125]{2,0,1:T(8,128)S(1)}, f32[16,128,125]{2,0,1:T(8,128)}, u32[]{:S(2)}) copy-start(f32[16,128,125]{2,0,1:T(8,128)} %copy.43) | copy-start | bytes 3072004
  147.0 11.7 %copy-start.13 = (s32[125,128]{0,1:T(8,128)S(1)}, s32[125,128]{0,1:T(8,128)}, u32[]{:S(2)}) copy-start(s32[125,128]{0,1:T(8,128)} %copy-done.10) | copy-start | bytes 192004
  147.0 11.7 %copy-start.15 = (f32[125,128]{0,1:T(8,128)S(1)}, f32[125,128]{0,1:T(8,128)}, u32[]{:S(2)}) copy-start(f32[125,128]{0,1:T(8,128)} %copy.21) | copy-start | bytes 192004
  147.0 11.7 %copy-start.18 = (f32[16,125,128]{1,0,2:T(8,128)S(1)}, f32[16,125,128]{1,0,2:T(8,128)}, u32[]{:S(2)}) copy-start(f32[16,125,128]{1,0,2:T(8,128)} %get-tuple-element.81) | copy-start | bytes 3072004
  158.8 9.9 %copy-start.17 = (f32[16,125,128]{1,0,2:T(8,128)S(1)}, f32[16,125,128]{1,0,2:T(8,128)}, u32[]{:S(2)}) copy-start(f32[16,125,128]{1,0,2:T(8,128)} %get-tuple-element.79) | copy-start | bytes 3072004
  168.6 10.1 %copy-start.16 = (f32[16,125,128]{1,0,2:T(8,128)S(1)}, f32[16,125,128]{1,0,2:T(8,128)}, u32[]{:S(2)}) copy-start(f32[16,125,128]{1,0,2:T(8,128)} %get-tuple-element.77) | copy-start | bytes 3072004
  199.4 10.9 %copy-start.3 = (bf16[16,32768]{1,0:T(8,128)(2,1)S(1)}, bf16[16,32768]{1,0:T(8,128)(2,1)}, u32[]{:S(2)}) copy-start(bf16[16,32768]{1,0:T(8,128)(2,1)} %param.12) | copy-start | bytes 3145732
  199.4 10.9 %copy-start.5 = (bf16[16,32768]{1,0:T(8,128)(2,1)S(1)}, bf16[16,32768]{1,0:T(8,128)(2,1)}, u32[]{:S(2)}) copy-start(bf16[16,32768]{1,0:T(8,128)(2,1)} %copy-done.4) | copy-start | bytes 3145732
  199.4 8.9 %collective-permute-start.6 = (bf16[16,8192]{1,0:T(8,128)(2,1)S(1)}, bf16[16,8192]{1,0:T(8,128)(2,1)S(1)}, u32[]{:S(2)}, u32[]{:S(2)}) collective-permute-start(bf16[16,8192]{1,0:T(8,128)(2,1)S(1)} %get-tuple-element.53), channel_id=1, source_target_pairs={{4,0},{8,4},{12,8},{16,12},{20,16},{24,20},{28,24},{32,28},{36,32}... | collective-permute-start | bytes 786440 | tf_op jit(solution)/shard_map/ppermute | solution.py:26
  201.0 8.4 %collective-permute-start.7 = (bf16[16,8192]{1,0:T(8,128)(2,1)S(1)}, bf16[16,8192]{1,0:T(8,128)(2,1)S(1)}, u32[]{:S(2)}, u32[]{:S(2)}) collective-permute-start(bf16[16,8192]{1,0:T(8,128)(2,1)S(1)} %get-tuple-element.52), channel_id=1, source_target_pairs={{0,4},{4,8},{8,12},{12,16},{16,20},{20,24},{24,28},{28,32},{32,36}... | collective-permute-start | bytes 786440 | tf_op jit(solution)/shard_map/ppermute | solution.py:26
Sparse Core Ops, SparseCore 0:
  211.9 75.0 all-gather.1
where the time goes:
time: 572 us; the launch traced here: 567 us
  blocking collectives  251 us (44%)
  matrix products  122 us (21%)
  waiting for transfers between devices  81.5 us (14%)
  local copies, waits for them, and re-layouts  37.1 us (6%)
  other arithmetic  33.2 us (6%)
  starting transfers between devices  27 us (5%)
  between operations  15.2 us (3%)
    psum x1, blocking collectives, per_device(): intersection = lax.psum(partial_intersection, 'node') / total_nodes  251 us
    dot_general x8, matrix products, cell_terms(): jnp.einsum('sjk,jkn->skn', mixed, picker.astype(jnp.float32), precision=l...  82.7 us
    all_gather x1, waiting for transfers between devices, per_device(): panel = lax.all_gather(second, 'state', axis=0, tiled=True)  75.3 us
    dot_general x8, matrix products, cell_terms(): jnp.einsum('skn,jkn->sjk', part_pair, picker_half, preferred_element_type...  27.9 us
    ppermute x4, starting transfers between devices, passed_along(): return lax.ppermute(block, axis, route)  16.9 us
  transfers between devices with their start and end apart: 9, of which 4 were waited for; matrix products, arithmetic and copies ran while one was open for 1% of the time, Pallas kernels for 0%

commit v1 on v0

--- a/solution.py
+++ b/solution.py
@@ -101,7 +101,8 @@
         jnp.bfloat16
     )
     total_nodes = block.shape[1] * lax.axis_size("node")
-    panel = lax.all_gather(second, "state", axis=0, tiled=True)
+    outgoing = jnp.stack([second] * lax.axis_size("state"))
+    panel = jnp.concatenate(lax.all_to_all(outgoing, "state", 0, 0), axis=0)
     partial_intersection = jnp.einsum("an,bn->ab", panel, panel, preferred_element_type=jnp.float32)
     intersection = lax.psum(partial_intersection, "node") / total_nodes
     factor, inverse = factorize(intersection)

time: 572 us -> 551 us (0.963)
  the two profiles are of different devices: /device:TPU:2 before, /device:TPU:128 now
where the time goes in v1:
time: 551 us; the launch traced here: 546 us
  blocking collectives  247 us (45%)
  matrix products  122 us (22%)
  waiting for transfers between devices  63.6 us (12%)
  starting transfers between devices  40.8 us (7%)
  local copies, waits for them, and re-layouts  39.4 us (7%)
  other arithmetic  32.2 us (6%)
    psum x1, blocking collectives, per_device(): intersection = lax.psum(partial_intersection, 'node') / total_nodes  247 us
    dot_general x8, matrix products, cell_terms(): jnp.einsum('sjk,jkn->skn', mixed, picker.astype(jnp.float32), precision=l...  82.7 us
    all_to_all x1, waiting for transfers between devices, per_device(): panel = jnp.concatenate(lax.all_to_all(outgoing, 'state', 0, 0), axis=0)  41.7 us
    dot_general x8, matrix products, cell_terms(): jnp.einsum('skn,jkn->sjk', part_pair, picker_half, preferred_element_type...  27.9 us
    ppermute x4, starting transfers between devices, passed_along(): return lax.ppermute(block, axis, route)  18.2 us
    ppermute x4, waiting for transfers between devices, passed_along(): return lax.ppermute(block, axis, route)  18 us
    ppermute x2, starting transfers between devices, extended(): lax.ppermute(lax.slice_in_dim(block, 0, width, axis=dim), axis, backward)  13.9 us
  transfers between devices with their start and end apart: 9, of which 7 were waited for; matrix products, arithmetic and copies ran while one was open for 1% of the time, Pallas kernels for 0%

profile of v1, /device:TPU:128, one launch (start us, length us, event | category | flops | bytes accessed | tf_op | source)
XLA Modules:
  0.0 546.2 jit_solution(17650693762845858804)
XLA Ops:
  1.8 1.9 collective-permute-start
  3.7 7.0 %collective-permute-start.1 = (bf16[16,8192]{1,0:T(8,128)(2,1)S(1)}, bf16[16,8192]{1,0:T(8,128)(2,1)S(1)}, u32[]{:S(2)}, u32[]{:S(2)}) collective-permute-start(bf16[16,8192]{1,0:T(8,128)(2,1)S(1)} %get-tuple-element.59), channel_id=1, source_target_pairs={{4,0},{8,4},{12,8},{16,12},{20,16},{24,20},{28,24},{32,28},{36,32}... | collective-permute-start | bytes 786440 | tf_op jit(solution)/shard_map/ppermute | solution.py:18
  16.1 3.2 reshape.137
  21.0 2.8 fusion.34
  23.8 3.0 fusion.123
  27.7 4.3 fusion.122
  32.8 4.3 fusion.121
  37.5 1.5 copy.37
  39.0 4.2 fusion.120
  45.0 11.6 %fusion.42 = f32[16,128,192]{2,0,1:T(8,128)S(1)} fusion(s32[125,128]{0,1:T(8,128)S(1)} %copy.16, f32[16,128,125]{2,0,1:T(8,128)S(1)} %copy.33, f32[16,125,128]{1,0,2:T(8,128)} %get-tuple-element.75, f32[125,128]{0,1:T(8,128)} %copy.19), kind=kOutput, calls=%fused_computation.59 | convolution fusion | flops 593408000 | bytes 3748864 | tf_op jit(solution)/shard_map/sjk,jkn->skn/dot_general | solution.py:58
  56.6 9.9 %fusion.44 = f32[16,128,192]{2,0,1:T(8,128)S(1)} fusion(s32[125,128]{0,1:T(8,128)S(1)} %copy-done.11, f32[16,128,125]{2,0,1:T(8,128)S(1)} %copy.35, f32[16,125,128]{1,0,2:T(8,128)S(1)} %copy-done.19, f32[125,128]{0,1:T(8,128)S(1)} %copy-done.14), kind=kOutput, calls=%fused_computation.61 | convolution fusion | flops 593408000 | bytes 3748864 | tf_op jit(solution)/shard_map/sjk,jkn->skn/dot_general | solution.py:58
  66.5 10.0 %fusion.46 = f32[16,128,192]{2,0,1:T(8,128)S(1)} fusion(s32[125,128]{0,1:T(8,128)S(1)} %copy.22, f32[16,128,125]{2,0,1:T(8,128)S(1)} %copy-done.7, f32[16,125,128]{1,0,2:T(8,128)S(1)} %copy-done.20, f32[125,128]{0,1:T(8,128)S(1)} %copy.23), kind=kOutput, calls=%fused_computation.63 | convolution fusion | flops 593408000 | bytes 3748864 | tf_op jit(solution)/shard_map/sjk,jkn->skn/dot_general | solution.py:58
  76.5 9.8 %fusion.48 = f32[16,128,192]{2,0,1:T(8,128)S(1)} fusion(s32[125,128]{0,1:T(8,128)S(1)} %copy.24, f32[16,128,125]{2,0,1:T(8,128)S(1)} %copy-done.9, f32[16,125,128]{1,0,2:T(8,128)S(1)} %copy-done.21, f32[125,128]{0,1:T(8,128)S(1)} %copy.25), kind=kOutput, calls=%fused_computation.65 | convolution fusion | flops 593408000 | bytes 3748864 | tf_op jit(solution)/shard_map/sjk,jkn->skn/dot_general | solution.py:58
  87.4 2.3 fusion.37
  89.7 3.2 copy.26
  93.0 4.0 reshape.138
  97.2 6.9 %collective-permute-start.2 = (bf16[16,8192]{1,0:T(8,128)(2,1)S(1)}, bf16[16,8192]{1,0:T(8,128)(2,1)S(1)}, u32[]{:S(2)}, u32[]{:S(2)}) collective-permute-start(bf16[16,8192]{1,0:T(8,128)(2,1)S(1)} %get-tuple-element.55), channel_id=1, source_target_pairs={{4,0},{8,4},{12,8},{16,12},{20,16},{24,20},{28,24},{32,28},{36,32}... | collective-permute-start | bytes 786440 | tf_op jit(solution)/shard_map/ppermute | solution.py:26
  104.9 2.1 collective-permute-start.3
  108.1 8.0 %collective-permute-done.3 = bf16[16,8192]{1,0:T(8,128)(2,1)S(1)} collective-permute-done((bf16[16,8192]{1,0:T(8,128)(2,1)S(1)}, bf16[16,8192]{1,0:T(8,128)(2,1)S(1)}, u32[]{:S(2)}, u32[]{:S(2)}) %collective-permute-start.3) | collective-permute-done | bytes 262176 | tf_op jit(solution)/shard_map/ppermute | solution.py:26
  117.3 1.9 collective-permute-start.4
  119.2 7.0 %collective-permute-start.5 = (bf16[16,8192]{1,0:T(8,128)(2,1)S(1)}, bf16[16,8192]{1,0:T(8,128)(2,1)S(1)}, u32[]{:S(2)}, u32[]{:S(2)}) collective-permute-start(bf16[16,8192]{1,0:T(8,128)(2,1)S(1)} %get-tuple-element.57), channel_id=1, source_target_pairs={{4,0},{8,4},{12,8},{16,12},{20,16},{24,20},{28,24},{32,28},{36,32}... | collective-permute-start | bytes 786440 | tf_op jit(solution)/shard_map/ppermute | solution.py:18
  126.2 2.1 collective-permute-done.4
  128.3 1.8 collective-permute-done.5
  131.3 3.2 reshape.139
  136.2 3.0 fusion.35
  139.2 3.0 fusion.127
  142.3 3.0 fusion.126
  145.3 3.0 fusion.125
  148.3 3.0 fusion.124
  156.7 11.7 %fusion.43 = f32[16,128,192]{2,0,1:T(8,128)S(1)} fusion(s32[125,128]{0,1:T(8,128)S(1)} %copy.16, f32[16,128,125]{2,0,1:T(8,128)} %copy.41, f32[16,125,128]{1,0,2:T(8,128)} %get-tuple-element.83, f32[125,128]{0,1:T(8,128)} %copy.19), kind=kOutput, calls=%fused_computation.60 | convolution fusion | flops 593408000 | bytes 3748864 | tf_op jit(solution)/shard_map/sjk,jkn->skn/dot_general | solution.py:58
  168.4 9.9 %fusion.45 = f32[16,128,192]{2,0,1:T(8,128)S(1)} fusion(s32[125,128]{0,1:T(8,128)S(1)} %copy-done.13, f32[16,128,125]{2,0,1:T(8,128)S(1)} %copy-done.8, f32[16,125,128]{1,0,2:T(8,128)S(1)} %copy-done.18, f32[125,128]{0,1:T(8,128)S(1)} %copy-done.15), kind=kOutput, calls=%fused_computation.62 | convolution fusion | flops 593408000 | bytes 3748864 | tf_op jit(solution)/shard_map/sjk,jkn->skn/dot_general | solution.py:58
  178.3 10.0 %fusion.47 = f32[16,128,192]{2,0,1:T(8,128)S(1)} fusion(s32[125,128]{0,1:T(8,128)S(1)} %copy.22, f32[16,128,125]{2,0,1:T(8,128)S(1)} %copy.45, f32[16,125,128]{1,0,2:T(8,128)S(1)} %copy-done.17, f32[125,128]{0,1:T(8,128)S(1)} %copy.23), kind=kOutput, calls=%fused_computation.64 | convolution fusion | flops 593408000 | bytes 3748864 | tf_op jit(solution)/shard_map/sjk,jkn->skn/dot_general | solution.py:58
  188.3 9.8 %fusion.49 = f32[16,128,192]{2,0,1:T(8,128)S(1)} fusion(s32[125,128]{0,1:T(8,128)S(1)} %copy.24, f32[16,128,125]{2,0,1:T(8,128)S(1)} %copy.47, f32[16,125,128]{1,0,2:T(8,128)S(1)} %copy-done.16, f32[125,128]{0,1:T(8,128)S(1)} %copy.25), kind=kOutput, calls=%fused_computation.66 | convolution fusion | flops 593408000 | bytes 3748864 | tf_op jit(solution)/shard_map/sjk,jkn->skn/dot_general | solution.py:58
  199.3 2.3 fusion.36
  201.6 3.2 copy.29
  204.8 4.0 reshape.140
  209.1 7.3 %collective-permute-start.6 = (bf16[16,8192]{1,0:T(8,128)(2,1)S(1)}, bf16[16,8192]{1,0:T(8,128)(2,1)S(1)}, u32[]{:S(2)}, u32[]{:S(2)}) collective-permute-start(bf16[16,8192]{1,0:T(8,128)(2,1)S(1)} %get-tuple-element.53), channel_id=1, source_target_pairs={{4,0},{8,4},{12,8},{16,12},{20,16},{24,20},{28,24},{32,28},{36,32}... | collective-permute-start | bytes 786440 | tf_op jit(solution)/shard_map/ppermute | solution.py:26
  216.5 1.9 collective-permute-start.7
  218.4 1.8 collective-permute-done.6
  220.3 7.2 %collective-permute-done.7 = bf16[16,8192]{1,0:T(8,128)(2,1)S(1)} collective-permute-done((bf16[16,8192]{1,0:T(8,128)(2,1)S(1)}, bf16[16,8192]{1,0:T(8,128)(2,1)S(1)}, u32[]{:S(2)}, u32[]{:S(2)}) %collective-permute-start.7) | collective-permute-done | bytes 262176 | tf_op jit(solution)/shard_map/ppermute | solution.py:26
  228.8 2.3 stack.2
  231.1 4.8 all-to-all-start
  235.9 41.7 %all-to-all-done = bf16[4,16,32768]{2,1,0:T(8,128)(2,1)} async-done(((bf16[4,16,32768]{2,1,0:T(8,128)(2,1)}), bf16[4,16,32768]{2,1,0:T(8,128)(2,1)}, u32[]{:S(2)}, u32[]{:S(2)}) %all-to-all-start) | async-done | bytes 4194336 | tf_op jit(solution)/shard_map/all_to_all | solution.py:105
  277.7 4.7 fusion.128
  282.4 246.6 %psum.7 = f32[64,64]{0,1:T(8,128)S(1)} all-reduce(f32[64,64]{0,1:T(8,128)S(1)} %fusion.128), channel_id=1, replica_groups=mesh['node'=64,'state'=4] {'node'}, use_global_device_ids=true, to_apply=%region_1.0 | all-reduce | flops 4096 | bytes 32768 | tf_op jit(solution)/shard_map/psum | solution.py:107
  529.0 5.8 %cholesky.17 = f32[64,64]{1,0:T(8,128)S(1)} custom-call(f32[64,64]{1,0:T(8,128)S(1)} %fusion.104), custom_call_target="Cholesky" | custom-call | tf_op jit(solution)/shard_map/jit(cholesky)/cholesky | solution.py:87
  536.8 4.9 custom-call.6
  542.0 3.8 convolution_convert_fusion
  (104 shorter events, 29.5 us)
Async XLA Ops:
  0.6 26.2 %copy-start = (bf16[125,125]{1,0:T(8,128)(2,1)S(1)}, bf16[125,125]{1,0:T(8,128)(2,1)}, u32[]{:S(2)}) copy-start(bf16[125,125]{1,0:T(8,128)(2,1)} %param.15) | copy-start | bytes 93754
  0.6 14.1 %copy-start.1 = (bf16[16,32768]{1,0:T(8,128)(2,1)S(1)}, bf16[16,32768]{1,0:T(8,128)(2,1)}, u32[]{:S(2)}) copy-start(bf16[16,32768]{1,0:T(8,128)(2,1)} %param.12) | copy-start | bytes 3145732
  1.8 12.9 %collective-permute-start = (bf16[16,8192]{1,0:T(8,128)(2,1)S(1)}, bf16[16,8192]{1,0:T(8,128)(2,1)S(1)}, u32[]{:S(2)}, u32[]{:S(2)}) collective-permute-start(bf16[16,8192]{1,0:T(8,128)(2,1)S(1)} %get-tuple-element.58), channel_id=1, source_target_pairs={{0,4},{4,8},{8,12},{12,16},{16,20},{20,24},{24,28},{28,32},{32,36}... | collective-permute-start | bytes 786440 | tf_op jit(solution)/shard_map/ppermute | solution.py:15
  3.7 11.0 %collective-permute-start.1 = (bf16[16,8192]{1,0:T(8,128)(2,1)S(1)}, bf16[16,8192]{1,0:T(8,128)(2,1)S(1)}, u32[]{:S(2)}, u32[]{:S(2)}) collective-permute-start(bf16[16,8192]{1,0:T(8,128)(2,1)S(1)} %get-tuple-element.59), channel_id=1, source_target_pairs={{4,0},{8,4},{12,8},{16,12},{20,16},{24,20},{28,24},{32,28},{36,32}... | collective-permute-start | bytes 786440 | tf_op jit(solution)/shard_map/ppermute | solution.py:18
  13.6 14.1 %copy-start.10 = (s32[125,128]{0,1:T(8,128)}, s32[125,128]{0,1:T(8,128)S(1)}, u32[]{:S(2)}) copy-start(s32[125,128]{0,1:T(8,128)S(1)} %copy.20) | copy-start | bytes 192004
  23.8 3.0 copy-start.6
  45.0 11.6 %copy-start.11 = (s32[125,128]{0,1:T(8,128)S(1)}, s32[125,128]{0,1:T(8,128)}, u32[]{:S(2)}) copy-start(s32[125,128]{0,1:T(8,128)} %copy-done.10) | copy-start | bytes 192004
  45.0 11.6 %copy-start.14 = (f32[125,128]{0,1:T(8,128)S(1)}, f32[125,128]{0,1:T(8,128)}, u32[]{:S(2)}) copy-start(f32[125,128]{0,1:T(8,128)} %copy.21) | copy-start | bytes 192004
  45.0 11.6 %copy-start.19 = (f32[16,125,128]{1,0,2:T(8,128)S(1)}, f32[16,125,128]{1,0,2:T(8,128)}, u32[]{:S(2)}) copy-start(f32[16,125,128]{1,0,2:T(8,128)} %get-tuple-element.73) | copy-start | bytes 3072004
  56.6 9.9 %copy-start.7 = (f32[16,128,125]{2,0,1:T(8,128)S(1)}, f32[16,128,125]{2,0,1:T(8,128)}, u32[]{:S(2)}) copy-start(f32[16,128,125]{2,0,1:T(8,128)} %copy.37) | copy-start | bytes 3072004
  56.6 9.9 %copy-start.20 = (f32[16,125,128]{1,0,2:T(8,128)S(1)}, f32[16,125,128]{1,0,2:T(8,128)}, u32[]{:S(2)}) copy-start(f32[16,125,128]{1,0,2:T(8,128)} %get-tuple-element.71) | copy-start | bytes 3072004
  66.5 10.0 %copy-start.9 = (f32[16,128,125]{2,0,1:T(8,128)S(1)}, f32[16,128,125]{2,0,1:T(8,128)}, u32[]{:S(2)}) copy-start(f32[16,128,125]{2,0,1:T(8,128)} %copy.39) | copy-start | bytes 3072004
  66.5 10.0 %copy-start.21 = (f32[16,125,128]{1,0,2:T(8,128)S(1)}, f32[16,125,128]{1,0,2:T(8,128)}, u32[]{:S(2)}) copy-start(f32[16,125,128]{1,0,2:T(8,128)} %get-tuple-element.69) | copy-start | bytes 3072004
  97.2 10.8 %collective-permute-start.2 = (bf16[16,8192]{1,0:T(8,128)(2,1)S(1)}, bf16[16,8192]{1,0:T(8,128)(2,1)S(1)}, u32[]{:S(2)}, u32[]{:S(2)}) collective-permute-start(bf16[16,8192]{1,0:T(8,128)(2,1)S(1)} %get-tuple-element.55), channel_id=1, source_target_pairs={{4,0},{8,4},{12,8},{16,12},{20,16},{24,20},{28,24},{32,28},{36,32}... | collective-permute-start | bytes 786440 | tf_op jit(solution)/shard_map/ppermute | solution.py:26
  104.8 12.1 %copy-start.2 = (bf16[16,32768]{1,0:T(8,128)(2,1)S(1)}, bf16[16,32768]{1,0:T(8,128)(2,1)}, u32[]{:S(2)}) copy-start(bf16[16,32768]{1,0:T(8,128)(2,1)} %param.12) | copy-start | bytes 3145732
  104.9 11.1 %collective-permute-start.3 = (bf16[16,8192]{1,0:T(8,128)(2,1)S(1)}, bf16[16,8192]{1,0:T(8,128)(2,1)S(1)}, u32[]{:S(2)}, u32[]{:S(2)}) collective-permute-start(bf16[16,8192]{1,0:T(8,128)(2,1)S(1)} %get-tuple-element.54), channel_id=1, source_target_pairs={{0,4},{4,8},{8,12},{12,16},{16,20},{20,24},{24,28},{28,32},{32,36}... | collective-permute-start | bytes 786440 | tf_op jit(solution)/shard_map/ppermute | solution.py:26
  117.2 12.8 %copy-start.4 = (bf16[16,32768]{1,0:T(8,128)(2,1)}, bf16[16,32768]{1,0:T(8,128)(2,1)S(1)}, u32[]{:S(2)}) copy-start(bf16[16,32768]{1,0:T(8,128)(2,1)S(1)} %fusion.40) | copy-start | bytes 3145732
  117.3 11.0 %collective-permute-start.4 = (bf16[16,8192]{1,0:T(8,128)(2,1)S(1)}, bf16[16,8192]{1,0:T(8,128)(2,1)S(1)}, u32[]{:S(2)}, u32[]{:S(2)}) collective-permute-start(bf16[16,8192]{1,0:T(8,128)(2,1)S(1)} %get-tuple-element.56), channel_id=1, source_target_pairs={{0,4},{4,8},{8,12},{12,16},{16,20},{20,24},{24,28},{28,32},{32,36}... | collective-permute-start | bytes 786440 | tf_op jit(solution)/shard_map/ppermute | solution.py:15
  119.2 10.8 %collective-permute-start.5 = (bf16[16,8192]{1,0:T(8,128)(2,1)S(1)}, bf16[16,8192]{1,0:T(8,128)(2,1)S(1)}, u32[]{:S(2)}, u32[]{:S(2)}) collective-permute-start(bf16[16,8192]{1,0:T(8,128)(2,1)S(1)} %get-tuple-element.57), channel_id=1, source_target_pairs={{4,0},{8,4},{12,8},{16,12},{20,16},{24,20},{28,24},{32,28},{36,32}... | collective-permute-start | bytes 786440 | tf_op jit(solution)/shard_map/ppermute | solution.py:18
  139.2 3.1 copy-start.12
  156.6 11.7 %copy-start.8 = (f32[16,128,125]{2,0,1:T(8,128)S(1)}, f32[16,128,125]{2,0,1:T(8,128)}, u32[]{:S(2)}) copy-start(f32[16,128,125]{2,0,1:T(8,128)} %copy.43) | copy-start | bytes 3072004
  156.6 11.7 %copy-start.13 = (s32[125,128]{0,1:T(8,128)S(1)}, s32[125,128]{0,1:T(8,128)}, u32[]{:S(2)}) copy-start(s32[125,128]{0,1:T(8,128)} %copy-done.10) | copy-start | bytes 192004
  156.6 11.7 %copy-start.15 = (f32[125,128]{0,1:T(8,128)S(1)}, f32[125,128]{0,1:T(8,128)}, u32[]{:S(2)}) copy-start(f32[125,128]{0,1:T(8,128)} %copy.21) | copy-start | bytes 192004
  156.7 11.7 %copy-start.18 = (f32[16,125,128]{1,0,2:T(8,128)S(1)}, f32[16,125,128]{1,0,2:T(8,128)}, u32[]{:S(2)}) copy-start(f32[16,125,128]{1,0,2:T(8,128)} %get-tuple-element.81) | copy-start | bytes 3072004
  168.4 9.9 %copy-start.17 = (f32[16,125,128]{1,0,2:T(8,128)S(1)}, f32[16,125,128]{1,0,2:T(8,128)}, u32[]{:S(2)}) copy-start(f32[16,125,128]{1,0,2:T(8,128)} %get-tuple-element.79) | copy-start | bytes 3072004
  178.3 10.1 %copy-start.16 = (f32[16,125,128]{1,0,2:T(8,128)S(1)}, f32[16,125,128]{1,0,2:T(8,128)}, u32[]{:S(2)}) copy-start(f32[16,125,128]{1,0,2:T(8,128)} %get-tuple-element.77) | copy-start | bytes 3072004
  209.0 19.3 %copy-start.3 = (bf16[16,32768]{1,0:T(8,128)(2,1)S(1)}, bf16[16,32768]{1,0:T(8,128)(2,1)}, u32[]{:S(2)}) copy-start(bf16[16,32768]{1,0:T(8,128)(2,1)} %param.12) | copy-start | bytes 3145732
  209.1 19.3 %copy-start.5 = (bf16[16,32768]{1,0:T(8,128)(2,1)S(1)}, bf16[16,32768]{1,0:T(8,128)(2,1)}, u32[]{:S(2)}) copy-start(bf16[16,32768]{1,0:T(8,128)(2,1)} %copy-done.4) | copy-start | bytes 3145732
  209.1 11.1 %collective-permute-start.6 = (bf16[16,8192]{1,0:T(8,128)(2,1)S(1)}, bf16[16,8192]{1,0:T(8,128)(2,1)S(1)}, u32[]{:S(2)}, u32[]{:S(2)}) collective-permute-start(bf16[16,8192]{1,0:T(8,128)(2,1)S(1)} %get-tuple-element.53), channel_id=1, source_target_pairs={{4,0},{8,4},{12,8},{16,12},{20,16},{24,20},{28,24},{32,28},{36,32}... | collective-permute-start | bytes 786440 | tf_op jit(solution)/shard_map/ppermute | solution.py:26
  216.5 11.0 %collective-permute-start.7 = (bf16[16,8192]{1,0:T(8,128)(2,1)S(1)}, bf16[16,8192]{1,0:T(8,128)(2,1)S(1)}, u32[]{:S(2)}, u32[]{:S(2)}) collective-permute-start(bf16[16,8192]{1,0:T(8,128)(2,1)S(1)} %get-tuple-element.52), channel_id=1, source_target_pairs={{0,4},{4,8},{8,12},{12,16},{16,20},{20,24},{24,28},{28,32},{32,36}... | collective-permute-start | bytes 786440 | tf_op jit(solution)/shard_map/ppermute | solution.py:26
  231.1 46.6 %all-to-all-start = ((bf16[4,16,32768]{2,1,0:T(8,128)(2,1)}), bf16[4,16,32768]{2,1,0:T(8,128)(2,1)}, u32[]{:S(2)}, u32[]{:S(2)}) async-start(bf16[4,16,32768]{2,1,0:T(8,128)(2,1)} %stack.2), calls=%async_computation | async-start | bytes 8388608 | tf_op jit(solution)/shard_map/all_to_all | solution.py:105
